TPU v7x, 32 devices: a whole 2x2x4 slice. The times are simulated.
32 devices in a mesh: dp: 8 (over z, x), tensor: 4 (over y, core).
Axes of the slice: x: 2, y: 2, z: 4, core: 2. Of those that a mesh axis runs over, the one named last changes fastest.
Arguments:
- frames: bfloat16 [2, 32768, 512], P(None, ('dp', 'tensor')), may hold values from -6 to 6
- cotangent: bfloat16 [2, 32768, 512], P(None, ('dp', 'tensor')), may hold values from -6 to 6
- clip_lengths: int32 [2, 32, 4], P(None, 'dp'), may hold values from 1 to 512, 1024 in all within a row
- in_proj: float32 [512, 8, 192], P('dp', 'tensor'), may hold values from -0.25 to 0.25
- out_proj: float32 [8, 64, 512], P('tensor', None, 'dp'), may hold values from -1 to 1
- up_proj: float32 [512, 2048], P('dp', 'tensor'), may hold values from -0.25 to 0.25
- down_proj: float32 [2048, 512], P('tensor', 'dp'), may hold values from -0.125 to 0.125
- small_params: float32 [6, 512], replicated, may hold values from 0.5 to 1.5
- in_first: float32 [512, 8, 192], P('dp', 'tensor'), may hold values from -384 to 384
- in_second: float32 [512, 8, 192], P('dp', 'tensor'), may hold values from 4194.304 to 16777.217
- out_first: float32 [8, 64, 512], P('tensor', None, 'dp'), may hold values from -128 to 128
- out_second: float32 [8, 64, 512], P('tensor', None, 'dp'), may hold values from 589.824 to 2359.296
- up_first: float32 [512, 2048], P('dp', 'tensor'), may hold values from -384 to 384
- up_second: float32 [512, 2048], P('dp', 'tensor'), may hold values from 4096 to 16384
- down_first: float32 [2048, 512], P('tensor', 'dp'), may hold values from -768 to 768
- down_second: float32 [2048, 512], P('tensor', 'dp'), may hold values from 16384 to 65536
- small_first: float32 [6, 512], replicated, may hold values from -1536 to 1536
- small_second: float32 [6, 512], replicated, may hold values from 65536 to 262144
Outputs:
- block_out: bfloat16 [2, 32768, 512], P(None, ('dp', 'tensor'))
- input_grad: bfloat16 [2, 32768, 512], P(None, ('dp', 'tensor'))
- in_new: float32 [512, 8, 192], P('dp', 'tensor')
- in_new_first: float32 [512, 8, 192], P('dp', 'tensor')
- in_new_second: float32 [512, 8, 192], P('dp', 'tensor')
- in_copy: bfloat16 [512, 8, 192], P('dp', 'tensor')
- out_new: float32 [8, 64, 512], P('tensor', None, 'dp')
- out_new_first: float32 [8, 64, 512], P('tensor', None, 'dp')
- out_new_second: float32 [8, 64, 512], P('tensor', None, 'dp')
- out_copy: bfloat16 [8, 64, 512], P('tensor', None, 'dp')
- up_new: float32 [512, 2048], P('dp', 'tensor')
- up_new_first: float32 [512, 2048], P('dp', 'tensor')
- up_new_second: float32 [512, 2048], P('dp', 'tensor')
- up_copy: bfloat16 [512, 2048], P('dp', 'tensor')
- down_new: float32 [2048, 512], P('tensor', 'dp')
- down_new_first: float32 [2048, 512], P('tensor', 'dp')
- down_new_second: float32 [2048, 512], P('tensor', 'dp')
- down_copy: bfloat16 [2048, 512], P('tensor', 'dp')
- small_grad: float32 [6, 512], replicated
- small_new: float32 [6, 512], replicated
- small_new_first: float32 [6, 512], replicated
- small_new_second: float32 [6, 512], replicated
- norms: float32 [2, 10], replicated
Inputs may be any that keep to these rules, and one draw needn't show every extreme that they name: `clip_lengths`: each bucket's 4 runs are whole numbers that sum to 1024; the last run of each bucket is padding.
All inputs are finite; a program needn't handle non-finite values.
Results may differ from a plain program's by a relative error of at most 0.015.
Values may be sent and summed in bfloat16 or wider, within the bound.
A program may use at most 256 MiB of HBM per device.

v0:
```python
import math
import jax
import jax.numpy as jnp
from jax import lax
from jax.sharding import PartitionSpec as P

D = 512
HEAD_DIM = 64
WINDOW = 250
LEN = 1024
CLIPS = 4
MICRO = 2
STEP = 3
beta_first = 0.5
beta_second = 0.5
adam_eps = 1e-06
decay_rate = 0.01
learn_rate = 0.3


def clip_layout(lengths):
    clip_ends = jnp.cumsum(lengths)
    position = jnp.arange(LEN, dtype=jnp.int32)
    clip_of = jnp.sum((position[:, None] >= clip_ends[None, : CLIPS - 1]).astype(jnp.int32), axis=1)
    starts = clip_ends - lengths
    belongs = clip_of[:, None] == jnp.arange(CLIPS, dtype=jnp.int32)[None, :]
    clip_begin = jnp.sum(jnp.where(belongs, starts[None, :], 0), axis=1)
    return (clip_of, position - clip_begin)


def allowed_pairs(clip_of):
    position = jnp.arange(LEN, dtype=jnp.int32)
    causal = position[None, :] <= position[:, None]
    inside = position[:, None] - position[None, :] < WINDOW
    same_clip = clip_of[:, None] == clip_of[None, :]
    return causal & inside & same_clip


def rotate(values_in, offset):
    half_dim = HEAD_DIM // 2
    frequency = jnp.exp(
        jnp.arange(half_dim, dtype=jnp.float32) * (-2.0 * math.log(10000.0) / HEAD_DIM)
    )
    angles = offset.astype(jnp.float32)[:, None] * frequency[None, :]
    cosine = jnp.cos(angles)
    sine = jnp.sin(angles)
    paired = values_in.reshape(values_in.shape[:-1] + (half_dim, 2))
    even_part = paired[..., 0]
    odd_part = paired[..., 1]
    turned = jnp.stack(
        [even_part * cosine - odd_part * sine, even_part * sine + odd_part * cosine], axis=-1
    )
    return turned.reshape(values_in.shape)


def layer_norm(rows, gain, bias):
    centred = rows - jnp.mean(rows, -1, keepdims=True)
    inverse = lax.rsqrt(jnp.mean(centred * centred, -1, keepdims=True) + 1e-05)
    normal = centred * inverse
    return (normal * gain + bias, normal, inverse)


def norm_back(incoming, normal, inverse, gain):
    scaled = incoming * gain
    return inverse * (
        scaled
        - jnp.mean(scaled, -1, keepdims=True)
        - normal * jnp.mean(scaled * normal, -1, keepdims=True)
    )


def gelu_value(values_in):
    return values_in * 0.5 * (1.0 + lax.erf(values_in * (1.0 / math.sqrt(2.0))))


def gelu_slope(values_in):
    cumulative = 0.5 * (1.0 + lax.erf(values_in * (1.0 / math.sqrt(2.0))))
    density = jnp.exp(-0.5 * values_in * values_in) * (1.0 / math.sqrt(2.0 * math.pi))
    return cumulative + values_in * density


def head_scores(queries, keys_rot, clip_of):
    raw = jnp.einsum("qd,kd->qk", queries, keys_rot, preferred_element_type=jnp.float32)
    return jnp.where(allowed_pairs(clip_of), raw * HEAD_DIM ** (-0.5), -1e30)


def attend_forward(head_item):
    head_part, clip_size = head_item
    clip_of, offset = clip_layout(clip_size)
    queries = rotate(head_part[:, 0], offset).astype(jnp.bfloat16)
    keys_rot = rotate(head_part[:, 1], offset).astype(jnp.bfloat16)
    values = head_part[:, 2].astype(jnp.bfloat16)
    scores = head_scores(queries, keys_rot, clip_of)
    top_score = jnp.max(scores, -1, keepdims=True)
    log_total = top_score + jnp.log(jnp.sum(jnp.exp(scores - top_score), -1, keepdims=True))
    attn = jnp.exp(scores - log_total)
    mixed_head = jnp.dot(
        attn.astype(jnp.bfloat16), values, preferred_element_type=jnp.float32
    ).astype(jnp.bfloat16)
    return (jnp.stack([queries, keys_rot, values]), log_total[:, 0], mixed_head)


def attend_back(head_item):
    kept_qkv, log_total, grad_head, clip_size = head_item
    clip_of, offset = clip_layout(clip_size)
    queries = kept_qkv[0]
    keys_rot = kept_qkv[1]
    values = kept_qkv[2]
    attn = jnp.exp(head_scores(queries, keys_rot, clip_of) - log_total[:, None])
    grad_values = jnp.einsum(
        "qk,qd->kd", attn.astype(jnp.bfloat16), grad_head, preferred_element_type=jnp.float32
    )
    grad_attn = jnp.einsum("qd,kd->qk", grad_head, values, preferred_element_type=jnp.float32)
    grad_scores = attn * (grad_attn - jnp.sum(grad_attn * attn, -1, keepdims=True))
    grad_raw = (grad_scores * HEAD_DIM ** (-0.5)).astype(jnp.bfloat16)
    grad_queries = jnp.dot(grad_raw, keys_rot, preferred_element_type=jnp.float32)
    grad_keys = jnp.einsum("qk,qd->kd", grad_raw, queries, preferred_element_type=jnp.float32)
    return jnp.stack(
        [rotate(grad_queries, -offset), rotate(grad_keys, -offset), grad_values], axis=1
    ).astype(jnp.bfloat16)


def split_heads(flat_rows, head_count, item_width):
    blocks = flat_rows.reshape(-1, LEN, head_count, item_width)
    return jnp.moveaxis(blocks, 2, 1).reshape(-1, LEN, item_width)


def merge_heads(head_items, head_count):
    item_width = head_items.shape[-1]
    blocks = head_items.reshape(-1, head_count, LEN, item_width)
    return jnp.moveaxis(blocks, 1, 2).reshape(-1, head_count * item_width)


def reduce_grads(local_grads):
    return (
        lax.psum_scatter(local_grads[0], "dp", scatter_dimension=0, tiled=True),
        lax.psum_scatter(local_grads[1], "dp", scatter_dimension=2, tiled=True),
        lax.psum_scatter(local_grads[2], "dp", scatter_dimension=0, tiled=True),
        lax.psum_scatter(local_grads[3], "dp", scatter_dimension=1, tiled=True),
    )


def on_device(
    frames,
    cotangent,
    clip_lengths,
    in_proj,
    out_proj,
    up_proj,
    down_proj,
    small_params,
    in_first,
    in_second,
    out_first,
    out_second,
    up_first,
    up_second,
    down_first,
    down_second,
    small_first,
    small_second,
):
    rows_here = frames.shape[1]
    own_buckets = rows_here // LEN
    first_bucket = lax.axis_index("tensor") * own_buckets
    copies = (
        in_proj.astype(jnp.bfloat16),
        out_proj.astype(jnp.bfloat16),
        up_proj.astype(jnp.bfloat16),
        down_proj.astype(jnp.bfloat16),
    )
    gathered = (
        lax.all_gather(copies[0], "dp", axis=0, tiled=True),
        lax.all_gather(copies[1], "dp", axis=2, tiled=True),
        lax.all_gather(copies[2], "dp", axis=0, tiled=True),
        lax.all_gather(copies[3], "dp", axis=1, tiled=True),
    )
    in_w, out_w, up_w, down_w = gathered
    head_count = in_w.shape[1]
    in_mat = in_w.reshape(D, -1)
    out_mat = out_w.reshape(-1, D)
    outputs = []
    input_grads = []
    small_terms = jnp.zeros((6, D), jnp.float32)
    owned = None
    for batch_index in range(MICRO):
        group_sizes = clip_lengths[batch_index]
        own_sizes = lax.dynamic_slice_in_dim(group_sizes, first_bucket, own_buckets, 0)
        rows_in = frames[batch_index].astype(jnp.float32)
        normed1, normal1, inverse1 = layer_norm(rows_in, small_params[0], small_params[1])
        enter1 = normed1.astype(jnp.bfloat16)
        enter1_all = lax.all_gather(enter1, "tensor", axis=0, tiled=True)
        projected = jnp.dot(enter1_all, in_mat, preferred_element_type=jnp.float32)
        head_items = split_heads(projected, head_count, 3 * HEAD_DIM).reshape(-1, LEN, 3, HEAD_DIM)
        item_sizes = jnp.repeat(group_sizes, head_count, axis=0)
        kept_qkv, log_totals, mixed_items = lax.map(attend_forward, (head_items, item_sizes))
        mixed_rows = merge_heads(mixed_items, head_count)
        branch = lax.psum_scatter(
            jnp.dot(mixed_rows, out_mat, preferred_element_type=jnp.float32),
            "tensor",
            scatter_dimension=0,
            tiled=True,
        )
        y_first = rows_in + small_params[4] * branch
        normed2, normal2, inverse2 = layer_norm(y_first, small_params[2], small_params[3])
        enter2 = normed2.astype(jnp.bfloat16)
        enter2_all = lax.all_gather(enter2, "tensor", axis=0, tiled=True)
        upval = jnp.dot(enter2_all, up_w, preferred_element_type=jnp.float32)
        act = gelu_value(upval).astype(jnp.bfloat16)
        mlp = lax.psum_scatter(
            jnp.dot(act, down_w, preferred_element_type=jnp.float32).astype(jnp.bfloat16),
            "tensor",
            scatter_dimension=0,
            tiled=True,
        ).astype(jnp.float32)
        outputs.append((y_first + small_params[5] * mlp).astype(jnp.bfloat16))
        clip_of = jax.vmap(lambda length_row: clip_layout(length_row)[0])(own_sizes)
        valid_rows = (clip_of < CLIPS - 1).astype(jnp.float32).reshape(-1)
        grad_y = cotangent[batch_index].astype(jnp.float32) * valid_rows[:, None]
        grad_mlp = (small_params[5] * grad_y).astype(jnp.bfloat16)
        grad_mlp_all = lax.all_gather(grad_mlp, "tensor", axis=0, tiled=True)
        grad_downproj = jnp.einsum(
            "rf,rd->fd", act, grad_mlp_all, preferred_element_type=jnp.float32
        )
        grad_act = jnp.einsum("rd,fd->rf", grad_mlp_all, down_w, preferred_element_type=jnp.float32)
        grad_up = (grad_act * gelu_slope(upval)).astype(jnp.bfloat16)
        grad_upproj = jnp.einsum(
            "rd,rf->df", enter2_all, grad_up, preferred_element_type=jnp.float32
        )
        grad_enter2 = lax.psum_scatter(
            jnp.einsum("rf,df->rd", grad_up, up_w, preferred_element_type=jnp.float32),
            "tensor",
            scatter_dimension=0,
            tiled=True,
        )
        grad_y_first = grad_y + norm_back(grad_enter2, normal2, inverse2, small_params[2])
        grad_branch = (small_params[4] * grad_y_first).astype(jnp.bfloat16)
        grad_branch_all = lax.all_gather(grad_branch, "tensor", axis=0, tiled=True)
        grad_outproj = jnp.einsum(
            "rh,rd->hd", mixed_rows, grad_branch_all, preferred_element_type=jnp.float32
        )
        grad_mixed = jnp.einsum(
            "rd,hd->rh", grad_branch_all, out_mat, preferred_element_type=jnp.float32
        ).astype(jnp.bfloat16)
        grad_items = split_heads(grad_mixed, head_count, HEAD_DIM)
        grad_heads = lax.map(attend_back, (kept_qkv, log_totals, grad_items, item_sizes))
        grad_projected = merge_heads(grad_heads.reshape(-1, LEN, 3 * HEAD_DIM), head_count)
        grad_inproj = jnp.einsum(
            "rd,re->de", enter1_all, grad_projected, preferred_element_type=jnp.float32
        )
        grad_enter1 = lax.psum_scatter(
            jnp.einsum(
                "re,de->rd", grad_projected, in_mat, preferred_element_type=jnp.float32
            ).astype(jnp.bfloat16),
            "tensor",
            scatter_dimension=0,
            tiled=True,
        ).astype(jnp.float32)
        grad_frames = grad_y_first + norm_back(grad_enter1, normal1, inverse1, small_params[0])
        input_grads.append(grad_frames.astype(jnp.bfloat16))
        small_terms = small_terms + jnp.stack(
            [
                jnp.sum(grad_enter1 * normal1, 0),
                jnp.sum(grad_enter1, 0),
                jnp.sum(grad_enter2 * normal2, 0),
                jnp.sum(grad_enter2, 0),
                jnp.sum(grad_y_first * branch, 0),
                jnp.sum(grad_y * mlp, 0),
            ]
        )
        micro_grads = (
            grad_inproj.reshape(in_w.shape),
            grad_outproj.reshape(out_w.shape),
            grad_upproj,
            grad_downproj,
        )
        summed = reduce_grads(micro_grads)
        owned = (
            summed if owned is None else tuple((left + right for left, right in zip(owned, summed)))
        )
    weights_in = (in_proj, out_proj, up_proj, down_proj)
    firsts = (in_first, out_first, up_first, down_first)
    seconds = (in_second, out_second, up_second, down_second)
    own_squares = jnp.stack([jnp.sum(weight * weight) for weight in weights_in])
    small_grad, weight_squares = lax.psum((small_terms, own_squares), ("dp", "tensor"))
    new_firsts = []
    new_seconds = []
    updates = []
    for weight, gradient, first, second in zip(weights_in, owned, firsts, seconds):
        first = beta_first * first + (1.0 - beta_first) * gradient
        second = beta_second * second + (1.0 - beta_second) * gradient * gradient
        update = (
            first
            / (1.0 - beta_first**STEP)
            / (jnp.sqrt(second / (1.0 - beta_second**STEP)) + adam_eps)
            + decay_rate * weight
        )
        new_firsts.append(first)
        new_seconds.append(second)
        updates.append(update)
    update_squares = lax.psum(
        jnp.stack([jnp.sum(update * update) for update in updates]), ("dp", "tensor")
    )
    trust_ratio = jnp.sqrt(weight_squares) * lax.rsqrt(update_squares + 1e-12)
    new_weights = [
        weights_in[index] - learn_rate * trust_ratio[index] * updates[index] for index in range(4)
    ]
    small_first_new = beta_first * small_first + (1.0 - beta_first) * small_grad
    small_second_new = beta_second * small_second + (1.0 - beta_second) * small_grad * small_grad
    small_update = (
        small_first_new
        / (1.0 - beta_first**STEP)
        / (jnp.sqrt(small_second_new / (1.0 - beta_second**STEP)) + adam_eps)
        + decay_rate * small_params
    )
    small_weight_sq = jnp.sum(small_params * small_params, axis=1, keepdims=True)
    small_update_sq = jnp.sum(small_update * small_update, axis=1, keepdims=True)
    small_new = (
        small_params
        - learn_rate * jnp.sqrt(small_weight_sq) * lax.rsqrt(small_update_sq + 1e-12) * small_update
    )
    norms = jnp.stack(
        [
            jnp.concatenate([jnp.sqrt(weight_squares), jnp.sqrt(small_weight_sq).reshape(-1)]),
            jnp.concatenate([jnp.sqrt(update_squares), jnp.sqrt(small_update_sq).reshape(-1)]),
        ]
    )
    block_out = jnp.stack(outputs)
    input_grad = jnp.stack(input_grads)
    return (
        block_out,
        input_grad,
        new_weights[0],
        new_firsts[0],
        new_seconds[0],
        new_weights[0].astype(jnp.bfloat16),
        new_weights[1],
        new_firsts[1],
        new_seconds[1],
        new_weights[1].astype(jnp.bfloat16),
        new_weights[2],
        new_firsts[2],
        new_seconds[2],
        new_weights[2].astype(jnp.bfloat16),
        new_weights[3],
        new_firsts[3],
        new_seconds[3],
        new_weights[3].astype(jnp.bfloat16),
        small_grad,
        small_new,
        small_first_new,
        small_second_new,
        norms,
    )


def solution(mesh):
    return jax.shard_map(
        on_device,
        mesh=mesh,
        in_specs=(
            P(None, ("dp", "tensor"), None),
            P(None, ("dp", "tensor"), None),
            P(None, "dp", None),
            P("dp", "tensor", None),
            P("tensor", None, "dp"),
            P("dp", "tensor"),
            P("tensor", "dp"),
            P(),
            P("dp", "tensor", None),
            P("dp", "tensor", None),
            P("tensor", None, "dp"),
            P("tensor", None, "dp"),
            P("dp", "tensor"),
            P("dp", "tensor"),
            P("tensor", "dp"),
            P("tensor", "dp"),
            P(),
            P(),
        ),
        out_specs=(
            P(None, ("dp", "tensor"), None),
            P(None, ("dp", "tensor"), None),
            P("dp", "tensor", None),
            P("dp", "tensor", None),
            P("dp", "tensor", None),
            P("dp", "tensor", None),
            P("tensor", None, "dp"),
            P("tensor", None, "dp"),
            P("tensor", None, "dp"),
            P("tensor", None, "dp"),
            P("dp", "tensor"),
            P("dp", "tensor"),
            P("dp", "tensor"),
            P("dp", "tensor"),
            P("tensor", "dp"),
            P("tensor", "dp"),
            P("tensor", "dp"),
            P("tensor", "dp"),
            P(),
            P(),
            P(),
            P(),
            P(),
        ),
        check_vma=False,
    )
```

profile of v0, /device:TPU:0, one launch (start us, length us, event | category | flops | bytes accessed | tf_op | source)
XLA Modules:
  0.0 1468.0 jit_solution(3563805246009885565)
XLA Ops:
  14.0 32.6 %all_gather.38 = bf16[2,64,512]{1,0,2:T(2,128)(2,1)S(1)} all-gather(bf16[2,64,64]{1,0,2:T(2,128)(2,1)S(1)} %copy.265), channel_id=1, replica_groups=mesh['dp'=8,'tensor'=4] {'dp'}, dimensions={2}, use_global_device_ids=true | all-gather | bytes 147456 | tf_op jit(solution)/shard_map/all_gather | solution.py:174
  48.0 31.3 %all_gather.37 = bf16[512,2,192]{2,1,0:T(2,128)(2,1)S(1)} all-gather(bf16[64,2,192]{2,1,0:T(2,128)(2,1)S(1)} %get-tuple-element.540), channel_id=1, replica_groups=mesh['dp'=8,'tensor'=4] {'dp'}, dimensions={0}, use_global_device_ids=true | all-gather | bytes 442368 | tf_op jit(solution)/shard_map/all_gather | solution.py:173
  80.4 6.8 fusion.222
  87.2 6.7 fusion.224
  98.3 124.4 %while.48 = (s32[]{:T(128)}, bf16[8,3,1024,64]{2,3,1,0:T(8,128)(2,1)}, f32[8,1024]{1,0:T(8,128)}, bf16[8,1024,64]{1,2,0:T(8,128)(2,1)}, f32[8,1024,3,64]{1,3,2,0...) while((s32[]{:T(128)}, bf16[8,3,1024,64]{2,3,1,0:T(8,128)(2,1)}, f32[8,1024]{1,0:T(8,128)}, ...), condition=%wide.region_8.9_spmd, body=%wide.region_2.8_spmd.sunk | while | flops 284020800 | bytes 21299740 | solution.py:196
  226.2 4.5 fusion.261
  235.7 124.8 %while.49 = (s32[]{:T(128)}, bf16[8,3,1024,64]{2,3,1,0:T(8,128)(2,1)}, f32[8,1024]{1,0:T(8,128)}, bf16[8,1024,64]{1,2,0:T(8,128)(2,1)}, f32[8,1024,3,64]{1,3,2,0...) while((s32[]{:T(128)}, bf16[8,3,1024,64]{2,3,1,0:T(8,128)(2,1)}, f32[8,1024]{1,0:T(8,128)}, ...), condition=%wide.region_21.22_spmd, body=%wide.region_15.21_spmd.sunk | while | flops 284020800 | bytes 21299740 | solution.py:196
  364.1 4.5 fusion.262
  368.7 72.5 %reduce-scatter.19.cloned.1.call-done = f32[1024,512]{1,0:T(8,128)} async-done(((f32[4096,512]{1,0:T(8,128)}), f32[1024,512]{1,0:T(8,128)}) %reduce-scatter.19.cloned.1.call-update) | async-done | bytes 2097168 | tf_op jit(solution)/shard_map/reduce_scatter | solution.py:198
  450.1 31.5 %all_gather.41 = bf16[512,512]{0,1:T(8,128)(2,1)S(1)} all-gather(bf16[512,64]{0,1:T(8,128)(2,1)S(1)} %convert_element_type.346), channel_id=1, replica_groups=mesh['dp'=8,'tensor'=4] {'dp'}, dimensions={1}, use_global_device_ids=true | all-gather | bytes 589824 | tf_op jit(solution)/shard_map/all_gather | solution.py:176
  481.6 31.6 %all_gather.40 = bf16[512,512]{1,0:T(8,128)(2,1)S(1)} all-gather(bf16[64,512]{1,0:T(8,128)(2,1)S(1)} %convert_element_type.344), channel_id=1, replica_groups=mesh['dp'=8,'tensor'=4] {'dp'}, dimensions={0}, use_global_device_ids=true | all-gather | bytes 589824 | tf_op jit(solution)/shard_map/all_gather | solution.py:175
  513.2 7.6 multiply_convert_fusion.3
  520.8 7.6 fusion.149
  530.4 5.8 fusion.263
  536.2 17.3 %all-gather.15.cloned.1.call-done = bf16[4096,512]{1,0:T(8,128)(2,1)} async-done(((bf16[1024,512]{1,0:T(8,128)(2,1)}), bf16[4096,512]{1,0:T(8,128)(2,1)}) %all-gather.15.cloned.1.call-update) | async-done | bytes 4194320 | tf_op jit(solution)/shard_map/all_gather | solution.py:207
  553.5 6.6 multiply_convert_fusion.2
  562.2 5.3 convolution_convert_fusion.2
  567.5 7.5 convolution_convert_fusion.3
  575.6 51.9 %reduce-scatter.23.cloned.1.call-done = f32[1024,512]{1,0:T(8,128)} async-done(((f32[4096,512]{1,0:T(8,128)}), f32[1024,512]{1,0:T(8,128)}) %reduce-scatter.23.cloned.1.call-update) | async-done | bytes 2097168 | tf_op jit(solution)/shard_map/reduce_scatter | solution.py:230
  630.7 44.0 %reduce-scatter.21.cloned.1.call-done = bf16[1024,512]{1,0:T(8,128)(2,1)} async-done(((bf16[4096,512]{1,0:T(8,128)(2,1)}), bf16[1024,512]{1,0:T(8,128)(2,1)}) %reduce-scatter.21.cloned.1.call-update) | async-done | bytes 1048592 | tf_op jit(solution)/shard_map/reduce_scatter | solution.py:210
  674.6 47.0 %reduce-scatter.17.cloned.1.call-done = bf16[1024,512]{1,0:T(8,128)(2,1)} async-done(((bf16[4096,512]{1,0:T(8,128)(2,1)}), bf16[1024,512]{1,0:T(8,128)(2,1)}) %reduce-scatter.17.cloned.1.call-update) | async-done | bytes 1048592 | tf_op jit(solution)/shard_map/reduce_scatter | solution.py:210
  721.6 6.3 fusion.201
  728.0 34.6 %all-gather.21.cloned.1.call-done = bf16[4096,512]{1,0:T(8,128)(2,1)} async-done(((bf16[1024,512]{1,0:T(8,128)(2,1)}), bf16[4096,512]{1,0:T(8,128)(2,1)}) %all-gather.21.cloned.1.call-update) | async-done | bytes 4194320 | tf_op jit(solution)/shard_map/all_gather | solution.py:221
  762.5 7.6 fusion.155
  772.1 5.8 fusion.264
  778.0 71.5 %reduce-scatter.27.cloned.1.call-done = f32[1024,512]{1,0:T(8,128)} async-done(((f32[4096,512]{1,0:T(8,128)}), f32[1024,512]{1,0:T(8,128)}) %reduce-scatter.27.cloned.1.call-update) | async-done | bytes 2097168 | tf_op jit(solution)/shard_map/reduce_scatter | solution.py:230
  852.9 4.0 multiply_reduce_fusion.2
  859.7 6.0 fusion.266
  869.3 5.9 fusion.265
  875.3 3.4 convolution_add_fusion.1
  879.1 14.4 all-gather.19.cloned.1.call-done
  893.5 3.4 convolution_convert_fusion.5
  899.1 30.3 %all-gather.23.cloned.1.call-done = bf16[4096,512]{1,0:T(8,128)(2,1)} async-done(((bf16[1024,512]{1,0:T(8,128)(2,1)}), bf16[4096,512]{1,0:T(8,128)(2,1)}) %all-gather.23.cloned.1.call-update) | async-done | bytes 4194320 | tf_op jit(solution)/shard_map/all_gather | solution.py:238
  929.4 3.4 convolution_convert_fusion.4
  940.0 100.4 %while.51 = (s32[]{:T(128)}, bf16[8,1024,3,64]{1,3,2,0:T(8,128)(2,1)}, s32[8,4]{1,0:T(8,128)}, bf16[8,3,1024,64]{2,3,1,0:T(8,128)(2,1)}, f32[8,1024]{1,0:T(8,128...) while((s32[]{:T(128)}, bf16[8,1024,3,64]{1,3,2,0:T(8,128)(2,1)}, ...), condition=%wide.region_50.51_spmd, body=%wide.region_45.50_spmd.sunk | while | flops 689820672 | bytes 37543496 | solution.py:246
  1040.5 3.6 copy.298
  1046.2 108.9 %while.50 = (s32[]{:T(128)}, bf16[8,1024,3,64]{1,3,2,0:T(8,128)(2,1)}, s32[8,4]{1,0:T(8,128)}, bf16[8,3,1024,64]{2,3,1,0:T(8,128)(2,1)}, f32[8,1024]{1,0:T(8,128...) while((s32[]{:T(128)}, bf16[8,1024,3,64]{1,3,2,0:T(8,128)(2,1)}, ...), condition=%wide.region_36.37_spmd, body=%wide.region_31.36_spmd.sunk | while | flops 689820672 | bytes 37543496 | solution.py:246
  1172.4 5.7 fusion.160
  1178.1 3.4 fusion.212
  1181.5 6.2 convolution_convert_fusion
  1188.1 4.4 convolution_convert_fusion.1
  1201.0 33.4 %reduce-scatter.37.cloned.1.call-done = f32[64,128]{1,0:T(8,128)} async-done(((f32[512,128]{1,0:T(8,128)}), f32[64,128]{1,0:T(8,128)}) %reduce-scatter.37.cloned.1.call-update) | async-done | bytes 32784
  1240.6 60.2 %reduce-scatter.31.cloned.1.call-done = f32[64,2,192]{2,0,1:T(8,128)} async-done(((f32[512,2,192]{2,0,1:T(8,128)}), f32[64,2,192]{2,0,1:T(8,128)}) %reduce-scatter.31.cloned.1.call-update) | async-done | bytes 98320 | tf_op jit(solution)/shard_map/reduce_scatter | solution.py:136
  1308.0 38.9 %reduce-scatter.29.cloned.1.call-done = bf16[1024,512]{1,0:T(8,128)(2,1)} async-done(((bf16[4096,512]{1,0:T(8,128)(2,1)}), bf16[1024,512]{1,0:T(8,128)(2,1)}) %reduce-scatter.29.cloned.1.call-update) | async-done | bytes 1048592 | tf_op jit(solution)/shard_map/reduce_scatter | solution.py:251
  1346.9 47.0 %reduce-scatter.25.cloned.1.call-done = bf16[1024,512]{1,0:T(8,128)(2,1)} async-done(((bf16[4096,512]{1,0:T(8,128)(2,1)}), bf16[1024,512]{1,0:T(8,128)(2,1)}) %reduce-scatter.25.cloned.1.call-update) | async-done | bytes 1048592 | tf_op jit(solution)/shard_map/reduce_scatter | solution.py:251
  1393.9 4.2 fusion.204
  1405.2 39.8 %all-reduce = (f32[4]{0:T(128)}, f32[4]{0:T(128)}, f32[6,512]{1,0:T(8,128)}) all-reduce(f32[4]{0:T(128)} %pad_maximum_fusion.8, f32[4]{0:T(128)} %pad_maximum_fusion.7, f32[6,512]{1,0:T(8,128)} %add.375), channel_id=1, replica_groups=mesh['dp'=8,'tensor'=4] {'dp','tensor'}, use_global_device_ids=true, to_apply=%region_71.72 | all-reduce | flops 3080 | bytes 24640 | tf_op jit(solution)/shard_map/psum | solution.py:301
  1451.3 4.2 fusion.220
  (1121 shorter events, 577.0 us)
Async XLA Ops:
  7.2 73.2 %all-gather.13.cloned.1.call-start = ((), (), s32[]{:S(2)}) async-start(), calls=%async_computation.16 | async-start | bytes 5242880 | tf_op jit(solution)/shard_map/all_gather | solution.py:192
  11.1 36.3 %copy-start.30 = (f32[64,2,192]{2,1,0:T(2,128)S(1)}, f32[64,2,192]{2,1,0:T(2,128)}, u32[]{:S(2)}) copy-start(f32[64,2,192]{2,1,0:T(2,128)} %param.29) | copy-start | bytes 294916
  13.0 66.8 %copy-start.67 = (s32[2,4,4]{2,1,0:T(4,128)S(1)}, s32[2,4,4]{2,1,0:T(4,128)}, u32[]{:S(2)}) copy-start(s32[2,4,4]{2,1,0:T(4,128)} %param.28) | copy-start | bytes 388
  13.0 74.2 %all-gather.9.cloned.1.call-start = ((), (), s32[]{:S(2)}) async-start(), calls=%async_computation.12 | async-start | bytes 5242880 | tf_op jit(solution)/shard_map/all_gather | solution.py:192
  13.8 354.8 %reduce-scatter.15.cloned.1.call-start = ((), (), s32[]{:S(2)}) async-start(), calls=%async_computation.13 | async-start | bytes 10485760 | tf_op jit(solution)/shard_map/reduce_scatter | solution.py:198
  79.8 7.4 copy-start.26
  230.7 210.4 %reduce-scatter.19.cloned.1.call-start = ((), (), s32[]{:S(2)}) async-start(), calls=%async_computation.17 | async-start | bytes 10485760 | tf_op jit(solution)/shard_map/reduce_scatter | solution.py:198
  368.6 72.6 %copy-start.61 = (f32[1,512]{1,0:T(1,128)S(1)}, f32[1,512]{1,0:T(1,128)}, u32[]{:S(2)}) copy-start(f32[1,512]{1,0:T(1,128)} %get-tuple-element.546) | copy-start | bytes 6148
  368.6 144.6 %all-gather.11.cloned.1.call-start = ((), (), s32[]{:S(2)}) async-start(), calls=%async_computation.14 | async-start | bytes 5242880 | tf_op jit(solution)/shard_map/all_gather | solution.py:207
  446.9 73.9 %all-gather.17.cloned.1.call-start = ((), (), s32[]{:S(2)}) async-start(), calls=%async_computation.20 | async-start | bytes 5242880 | tf_op jit(solution)/shard_map/all_gather | solution.py:221
  449.3 104.2 %all-gather.15.cloned.1.call-start = ((), (), s32[]{:S(2)}) async-start(), calls=%async_computation.18 | async-start | bytes 5242880 | tf_op jit(solution)/shard_map/all_gather | solution.py:207
  450.0 177.4 %reduce-scatter.23.cloned.1.call-start = ((), (), s32[]{:S(2)}) async-start(), calls=%async_computation.21 | async-start | bytes 10485760 | tf_op jit(solution)/shard_map/reduce_scatter | solution.py:230
  536.2 138.5 %reduce-scatter.21.cloned.1.call-start = ((), (), s32[]{:S(2)}) async-start(), calls=%async_computation.19 | async-start | bytes 5242880 | tf_op jit(solution)/shard_map/reduce_scatter | solution.py:210
  567.5 154.2 %reduce-scatter.17.cloned.1.call-start = ((), (), s32[]{:S(2)}) async-start(), calls=%async_computation.15 | async-start | bytes 5242880 | tf_op jit(solution)/shard_map/reduce_scatter | solution.py:210
  575.0 52.4 %copy-start.5 = (f32[1024,512]{1,0:T(8,128)S(1)}, f32[1024,512]{1,0:T(8,128)}, u32[]{:S(2)}) copy-start(f32[1024,512]{1,0:T(8,128)} %copy-done.4) | copy-start | bytes 6291460
  575.1 187.5 %all-gather.21.cloned.1.call-start = ((), (), s32[]{:S(2)}) async-start(), calls=%async_computation.24 | async-start | bytes 5242880 | tf_op jit(solution)/shard_map/all_gather | solution.py:221
  727.9 121.6 %reduce-scatter.27.cloned.1.call-start = ((), (), s32[]{:S(2)}) async-start(), calls=%async_computation.25 | async-start | bytes 10485760 | tf_op jit(solution)/shard_map/reduce_scatter | solution.py:230
  777.9 71.6 %copy-start.3 = (f32[1024,512]{1,0:T(8,128)S(1)}, f32[1024,512]{1,0:T(8,128)}, u32[]{:S(2)}) copy-start(f32[1024,512]{1,0:T(8,128)} %copy-done.2) | copy-start | bytes 6291460
  777.9 74.9 %copy-start.25 = (bf16[1024,512]{1,0:T(8,128)(2,1)S(1)}, bf16[1024,512]{1,0:T(8,128)(2,1)}, u32[]{:S(2)}) copy-start(bf16[1024,512]{1,0:T(8,128)(2,1)} %reduce-scatter.21.cloned.1.call-done) | copy-start | bytes 3145732
  778.0 115.5 %all-gather.19.cloned.1.call-start = ((), (), s32[]{:S(2)}) async-start(), calls=%async_computation.22 | async-start | bytes 5242880 | tf_op jit(solution)/shard_map/all_gather | solution.py:238
  852.9 4.0 copy-start.10
  858.9 70.5 %all-gather.23.cloned.1.call-start = ((), (), s32[]{:S(2)}) async-start(), calls=%async_computation.26 | async-start | bytes 5242880 | tf_op jit(solution)/shard_map/all_gather | solution.py:238
  859.5 333.1 %reduce-scatter.35.cloned.1.call-start = ((), (), s32[]{:S(2)}) async-start(), calls=%async_computation.30 | async-start | bytes 1179648 | tf_op jit(solution)/shard_map/reduce_scatter | solution.py:139
  859.7 6.0 copy-start.68
  859.7 6.2 copy-start.70
  869.3 326.5 %reduce-scatter.33.cloned.1.call-start = ((), (), s32[]{:S(2)}) async-start(), calls=%async_computation.29 | async-start | bytes 1179648 | tf_op jit(solution)/shard_map/reduce_scatter | solution.py:138
  869.3 6.0 copy-start.8
  869.3 6.0 copy-start.18
  878.7 355.7 %reduce-scatter.37.cloned.1.call-start = ((), (), s32[]{:S(2)}) async-start(), calls=%async_computation.31 | async-start | bytes 294912
  1046.2 108.9 %copy-start.13 = (bf16[16,8,4,1024]{3,1,2,0:T(8,128)(2,1)S(1)}, bf16[16,8,4,1024]{3,1,2,0:T(8,128)(2,1)}, u32[]{:S(2)}) copy-start(bf16[16,8,4,1024]{3,1,2,0:T(8,128)(2,1)} %copy-done.12) | copy-start | bytes 3145732
  1155.2 3.7 copy-start.15
  1158.9 3.8 copy-start.17
  1172.1 128.8 %reduce-scatter.31.cloned.1.call-start = ((), (), s32[]{:S(2)}) async-start(), calls=%async_computation.28 | async-start | bytes 1179648 | tf_op jit(solution)/shard_map/reduce_scatter | solution.py:136
  1172.4 5.7 copy-start.23
  1181.5 165.5 %reduce-scatter.29.cloned.1.call-start = ((), (), s32[]{:S(2)}) async-start(), calls=%async_computation.27 | async-start | bytes 5242880 | tf_op jit(solution)/shard_map/reduce_scatter | solution.py:251
  1187.8 206.1 %reduce-scatter.25.cloned.1.call-start = ((), (), s32[]{:S(2)}) async-start(), calls=%async_computation.23 | async-start | bytes 5242880 | tf_op jit(solution)/shard_map/reduce_scatter | solution.py:251
  1192.5 5.6 copy-start.24
  1192.5 108.4 %copy-start.31 = (f32[64,2,192]{2,1,0:T(2,128)S(1)}, f32[64,2,192]{2,1,0:T(2,128)}, u32[]{:S(2)}) copy-start(f32[64,2,192]{2,1,0:T(2,128)} %param.29) | copy-start | bytes 294916
  1198.1 195.8 %copy-start.1 = (bf16[2,1024,512]{2,1,0:T(8,128)(2,1)S(1)}, bf16[2,1024,512]{2,1,0:T(8,128)(2,1)}, u32[]{:S(2)}) copy-start(bf16[2,1024,512]{2,1,0:T(8,128)(2,1)} %param.26) | copy-start | bytes 6291460
  1198.1 195.8 %copy-start.51 = (f32[1024]{0:T(1024)S(1)}, f32[1024]{0:T(1024)}, u32[]{:S(2)}) copy-start(f32[1024]{0:T(1024)} %copy-done.50) | copy-start | bytes 12292
  1198.1 195.8 %copy-start.53 = (f32[1024]{0:T(1024)S(1)}, f32[1024]{0:T(1024)}, u32[]{:S(2)}) copy-start(f32[1024]{0:T(1024)} %copy-done.52) | copy-start | bytes 12292
  1198.1 195.8 %copy-start.57 = (f32[1024]{0:T(1024)S(1)}, f32[1024]{0:T(1024)}, u32[]{:S(2)}) copy-start(f32[1024]{0:T(1024)} %copy-done.56) | copy-start | bytes 12292
  1198.1 195.8 %copy-start.59 = (f32[1024]{0:T(1024)S(1)}, f32[1024]{0:T(1024)}, u32[]{:S(2)}) copy-start(f32[1024]{0:T(1024)} %copy-done.58) | copy-start | bytes 12292
  1346.9 104.4 %copy-start.22 = (bf16[1024,512]{1,0:T(8,128)(2,1)S(1)}, bf16[1024,512]{1,0:T(8,128)(2,1)}, u32[]{:S(2)}) copy-start(bf16[1024,512]{1,0:T(8,128)(2,1)} %reduce-scatter.29.cloned.1.call-done) | copy-start | bytes 3145732
  1455.6 3.9 copy-start.38
  1455.6 3.8 copy-start.39
  1455.6 4.6 copy-start.40
  1455.6 4.6 copy-start.41
  (43 other events, 111.8 us)
Sparse Core Ops, SparseCore 0:
  13.1 37.1 all-gather.12
  52.5 34.4 all-gather.8
  230.8 72.4 reduce-scatter.14
  368.7 72.3 reduce-scatter.18
  447.0 34.4 all-gather.10
  482.9 34.4 all-gather.16
  519.0 34.4 all-gather.14
  556.1 71.3 reduce-scatter.22
  630.0 44.5 reduce-scatter.20
  677.0 44.5 reduce-scatter.16
  728.0 34.4 all-gather.20
  778.1 71.3 reduce-scatter.26
  859.0 34.4 all-gather.18
  894.9 34.4 all-gather.22
  932.6 64.2 reduce-scatter.34
  1000.2 63.2 reduce-scatter.32
  1172.2 62.0 reduce-scatter.36
  1237.6 63.1 reduce-scatter.30
  1303.4 43.4 reduce-scatter.28
  1349.3 44.5 reduce-scatter.24
where the time goes:
time: 1480 us; the launch traced here: 1470 us
  waiting for transfers between devices  565 us (38%)
  matrix products  269 us (18%)
  local copies, waits for them, and re-layouts  228 us (15%)
  other arithmetic  216 us (15%)
  blocking collectives  167 us (11%)
  between operations  18.1 us (1%)
    reduce_scatter x2, waiting for transfers between devices, on_device(): lax.psum_scatter(jnp.einsum('rf,df->rd', grad_up, up_w, preferred_element...  123 us
    reduce_scatter x2, waiting for transfers between devices, on_device(): lax.psum_scatter(jnp.dot(act, down_w, preferred_element_type=jnp.float32)...  90.9 us
    reduce_scatter x2, waiting for transfers between devices, on_device(): lax.psum_scatter(jnp.einsum('re,de->rd', grad_projected, in_mat, preferre...  85.9 us
    reduce_scatter x2, waiting for transfers between devices, on_device(): lax.psum_scatter(jnp.dot(mixed_rows, out_mat, preferred_element_type=jnp....  72.5 us
    reduce_scatter x1, waiting for transfers between devices, reduce_grads(): lax.psum_scatter(local_grads[0], 'dp', scatter_dimension=0, tiled=True)  60.2 us
    dot_general x32, matrix products, head_scores(): jnp.einsum('qd,kd->qk', queries, keys_rot, preferred_element_type=jnp.flo...  53.3 us
    all_gather x2, waiting for transfers between devices, on_device(): grad_branch_all = lax.all_gather(grad_branch, 'tensor', axis=0, tiled=True)  44.6 us
    psum x1, blocking collectives, on_device(): lax.psum(jnp.stack([jnp.sum(update * update) for update in updates]), ('d...  39.8 us
  transfers between devices with their start and end apart: 20, of which 13 were waited for; matrix products, arithmetic and copies ran while one was open for 34% of the time, Pallas kernels for 0%

commit v1 on v0

--- a/solution.py
+++ b/solution.py
@@ -218,7 +218,38 @@
         valid_rows = (clip_of < CLIPS - 1).astype(jnp.float32).reshape(-1)
         grad_y = cotangent[batch_index].astype(jnp.float32) * valid_rows[:, None]
         grad_mlp = (small_params[5] * grad_y).astype(jnp.bfloat16)
-        grad_mlp_all = lax.all_gather(grad_mlp, "tensor", axis=0, tiled=True)
+
+        def serve_circles_in(payload, named_axis):
+            found_now = lax.axis_size(named_axis)
+            all_values = lax.axis_index(named_axis)
+            even, w_next, kept_arr = (found_now, all_values, payload.shape[0])
+            inbox = []
+            for it, t in enumerate(payload.shape):
+                inbox.append(t * even if it == 0 else t)
+            mixed_arr = jnp.zeros(inbox, payload.dtype)
+            piece_out = lax.dynamic_update_slice_in_dim(
+                mixed_arr, payload, w_next * kept_arr, axis=0
+            )
+            moved = shaped = payload
+            for c in range(1, even // 2 + 1):
+                trail = []
+                for it in range(even):
+                    trail.append((it, (it + 1) % even))
+                moved = lax.ppermute(moved, named_axis, trail)
+                piece_out = lax.dynamic_update_slice_in_dim(
+                    piece_out, moved, (w_next - c) % even * kept_arr, axis=0
+                )
+                if 2 * c < even:
+                    row_list = []
+                    for it in range(even):
+                        row_list.append((it, (it - 1) % even))
+                    shaped = lax.ppermute(shaped, named_axis, row_list)
+                    piece_out = lax.dynamic_update_slice_in_dim(
+                        piece_out, shaped, (w_next + c) % even * kept_arr, axis=0
+                    )
+            return piece_out
+
+        grad_mlp_all = serve_circles_in(grad_mlp, "tensor")
         grad_downproj = jnp.einsum(
             "rf,rd->fd", act, grad_mlp_all, preferred_element_type=jnp.float32
         )

time: 1480 us -> 1670 us (1.13)
  local copies, waits for them, and re-layouts: 228 us -> 308 us
  matrix products: 269 us -> 330 us
  waiting for transfers between devices: 565 us -> 611 us
    while x0 -> x128, local copies, waits for them, and re-layouts: none -> 69.1 us
    ppermute x0 -> x6, waiting for transfers between devices: none -> 67.3 us  [the longest x4 67.3 us: serve_circles_in(): moved = lax.ppermute(moved, named_axis, trail)]
    reduce_scatter x1, waiting for transfers between devices: 0.02 us -> 64.2 us  [reduce_grads(): lax.psum_scatter(local_grads[3], 'dp', scatter_dimension=1, tiled=True)]
    dot_general x16, matrix products: 23 us -> 57.7 us  [attend_forward(): jnp.dot(attn.astype(jnp.bfloat16), values, preferred_element_type=jnp.flo...]
    all_gather x2 -> x0, waiting for transfers between devices: 34.6 us -> none  [on_device(): grad_mlp_all = lax.all_gather(grad_mlp, 'tensor', axis=0, tiled=True)]
    dot_general x16, matrix products: 27.5 us -> 52.1 us  [attend_back(): jnp.einsum('qd,kd->qk', grad_head, values, preferred_element_type=jnp.flo...]
    all_gather x2, waiting for transfers between devices: 44.6 us -> 23.8 us  [on_device(): grad_branch_all = lax.all_gather(grad_branch, 'tensor', axis=0, tiled=True)]
    all_gather x2, waiting for transfers between devices: 17.3 us -> 0.02 us  [on_device(): enter2_all = lax.all_gather(enter2, 'tensor', axis=0, tiled=True)]
  transfers between devices with their start and end apart: 20 -> 24, of which waited for: 13 -> 14; matrix products, arithmetic and copies ran while one was open for 34% -> 42% of each run, Pallas kernels for 0% -> 0%
where the time goes in v1:
time: 1670 us; the launch traced here: 1650 us
  waiting for transfers between devices  611 us (37%)
  matrix products  330 us (20%)
  local copies, waits for them, and re-layouts  308 us (18%)
  other arithmetic  206 us (12%)
  blocking collectives  167 us (10%)
  between operations  18.2 us (1%)
    reduce_scatter x2, waiting for transfers between devices, on_device(): lax.psum_scatter(jnp.einsum('rf,df->rd', grad_up, up_w, preferred_element...  115 us
    reduce_scatter x2, waiting for transfers between devices, on_device(): lax.psum_scatter(jnp.einsum('re,de->rd', grad_projected, in_mat, preferre...  86.1 us
    reduce_scatter x2, waiting for transfers between devices, on_device(): lax.psum_scatter(jnp.dot(act, down_w, preferred_element_type=jnp.float32)...  83.9 us
    reduce_scatter x2, waiting for transfers between devices, on_device(): lax.psum_scatter(jnp.dot(mixed_rows, out_mat, preferred_element_type=jnp....  72.3 us
    while x128, local copies, waits for them, and re-layouts  69.1 us
    ppermute x4, waiting for transfers between devices, serve_circles_in(): moved = lax.ppermute(moved, named_axis, trail)  67.3 us
    reduce_scatter x1, waiting for transfers between devices, reduce_grads(): lax.psum_scatter(local_grads[3], 'dp', scatter_dimension=1, tiled=True)  64.2 us
    reduce_scatter x1, waiting for transfers between devices, reduce_grads(): lax.psum_scatter(local_grads[0], 'dp', scatter_dimension=0, tiled=True)  60 us
  transfers between devices with their start and end apart: 24, of which 14 were waited for; matrix products, arithmetic and copies ran while one was open for 42% of the time, Pallas kernels for 0%

profile of v1, /device:TPU:0, one launch (start us, length us, event | category | flops | bytes accessed | tf_op | source)
XLA Modules:
  0.0 1649.4 jit_solution(2800905554426025713)
XLA Ops:
  15.4 33.1 %all_gather.31 = bf16[512,2,192]{2,1,0:T(2,128)(2,1)S(1)} all-gather(bf16[64,2,192]{2,1,0:T(2,128)(2,1)S(1)} %get-tuple-element.543), channel_id=1, replica_groups=mesh['dp'=8,'tensor'=4] {'dp'}, dimensions={0}, use_global_device_ids=true | all-gather | bytes 442368 | tf_op jit(solution)/shard_map/all_gather | solution.py:173
  49.7 30.7 %all_gather.32 = bf16[2,64,512]{1,0,2:T(2,128)(2,1)S(1)} all-gather(bf16[2,64,64]{1,0,2:T(2,128)(2,1)S(1)} %copy.265), channel_id=1, replica_groups=mesh['dp'=8,'tensor'=4] {'dp'}, dimensions={2}, use_global_device_ids=true | all-gather | bytes 147456 | tf_op jit(solution)/shard_map/all_gather | solution.py:174
  81.3 6.7 fusion.222
  92.3 158.1 %while.49 = (s32[]{:T(128)}, bf16[8,3,1024,64]{2,3,1,0:T(8,128)(2,1)}, f32[8,1024]{1,0:T(8,128)}, bf16[8,1024,64]{1,2,0:T(8,128)(2,1)}, f32[8,1024,3,64]{1,3,2,0...) while((s32[]{:T(128)}, bf16[8,3,1024,64]{2,3,1,0:T(8,128)(2,1)}, f32[8,1024]{1,0:T(8,128)}, ...), condition=%wide.region_21.22_spmd, body=%wide.region_15.21_spmd.sunk | while | flops 284020800 | bytes 38076984 | solution.py:196
  253.9 4.5 fusion.266
  259.4 6.8 fusion.224
  270.3 147.3 %while.48 = (s32[]{:T(128)}, bf16[8,3,1024,64]{2,3,1,0:T(8,128)(2,1)}, f32[8,1024]{1,0:T(8,128)}, bf16[8,1024,64]{1,2,0:T(8,128)(2,1)}, f32[8,1024,3,64]{1,3,2,0...) while((s32[]{:T(128)}, bf16[8,3,1024,64]{2,3,1,0:T(8,128)(2,1)}, f32[8,1024]{1,0:T(8,128)}, ...), condition=%wide.region_8.9_spmd, body=%wide.region_2.8_spmd.sunk | while | flops 284020800 | bytes 38078064 | solution.py:196
  358.9 3.6 fusion.389
  377.3 3.6 fusion.389
  414.0 3.6 fusion.389
  421.1 4.5 fusion.265
  425.7 72.3 %reduce-scatter.15.cloned.1.call-done = f32[1024,512]{1,0:T(8,128)} async-done(((f32[4096,512]{1,0:T(8,128)}), f32[1024,512]{1,0:T(8,128)}) %reduce-scatter.15.cloned.1.call-update) | async-done | bytes 2097168 | tf_op jit(solution)/shard_map/reduce_scatter | solution.py:198
  516.0 34.9 %collective-permute-done = bf16[1024,512]{1,0:T(8,128)(2,1)} collective-permute-done((bf16[1024,512]{1,0:T(8,128)(2,1)}, bf16[1024,512]{1,0:T(8,128)(2,1)}, u32[]{:S(2)}, u32[]{:S(2)}) %collective-permute-start) | collective-permute-done | bytes 1048608 | tf_op jit(solution)/shard_map/ppermute | solution.py:238
  550.9 31.3 %collective-permute-done.3 = bf16[1024,512]{1,0:T(8,128)(2,1)S(1)} collective-permute-done((bf16[1024,512]{1,0:T(8,128)(2,1)}, bf16[1024,512]{1,0:T(8,128)(2,1)S(1)}, u32[]{:S(2)}, u32[]{:S(2)}) %collective-permute-start.3) | collective-permute-done | bytes 1048608 | tf_op jit(solution)/shard_map/ppermute | solution.py:238
  582.2 31.4 %all_gather.34 = bf16[512,512]{1,0:T(8,128)(2,1)S(1)} all-gather(bf16[64,512]{1,0:T(8,128)(2,1)S(1)} %convert_element_type.344), channel_id=1, replica_groups=mesh['dp'=8,'tensor'=4] {'dp'}, dimensions={0}, use_global_device_ids=true | all-gather | bytes 589824 | tf_op jit(solution)/shard_map/all_gather | solution.py:175
  627.2 6.7 multiply_convert_fusion.2
  638.2 6.6 multiply_convert_fusion.3
  646.8 5.6 convolution_add_fusion
  652.5 64.2 %reduce-scatter.35.cloned.1.call-done = f32[512,64]{0,1:T(8,128)} async-done(((f32[512,512]{0,1:T(8,128)}), f32[512,64]{0,1:T(8,128)}) %reduce-scatter.35.cloned.1.call-update) | async-done | bytes 131088 | tf_op jit(solution)/shard_map/reduce_scatter | solution.py:139
  719.0 31.7 %all_gather.35 = bf16[512,512]{0,1:T(8,128)(2,1)S(1)} all-gather(bf16[512,64]{0,1:T(8,128)(2,1)S(1)} %get-tuple-element.544), channel_id=1, replica_groups=mesh['dp'=8,'tensor'=4] {'dp'}, dimensions={1}, use_global_device_ids=true | all-gather | bytes 589824 | tf_op jit(solution)/shard_map/all_gather | solution.py:176
  750.7 7.6 fusion.149
  760.4 5.8 fusion.267
  766.3 7.7 fusion.155
  776.6 5.8 fusion.268
  782.4 6.6 convolution_convert_fusion.2
  789.4 6.5 convolution_convert_fusion.3
  795.9 40.5 %reduce-scatter.23.cloned.1.call-done = f32[1024,512]{1,0:T(8,128)} async-done(((f32[4096,512]{1,0:T(8,128)}), f32[1024,512]{1,0:T(8,128)}) %reduce-scatter.23.cloned.1.call-update) | async-done | bytes 2097168 | tf_op jit(solution)/shard_map/reduce_scatter | solution.py:261
  836.5 74.0 %reduce-scatter.27.cloned.1.call-done = f32[1024,512]{1,0:T(8,128)} async-done(((f32[4096,512]{1,0:T(8,128)}), f32[1024,512]{1,0:T(8,128)}) %reduce-scatter.27.cloned.1.call-update) | async-done | bytes 2097168 | tf_op jit(solution)/shard_map/reduce_scatter | solution.py:261
  910.5 4.4 multiply_reduce_fusion.5
  914.9 42.6 %reduce-scatter.21.cloned.1.call-done = bf16[1024,512]{1,0:T(8,128)(2,1)} async-done(((bf16[4096,512]{1,0:T(8,128)(2,1)}), bf16[1024,512]{1,0:T(8,128)(2,1)}) %reduce-scatter.21.cloned.1.call-update) | async-done | bytes 1048592 | tf_op jit(solution)/shard_map/reduce_scatter | solution.py:210
  957.4 5.8 multiply_reduce_fusion.2
  963.3 41.3 %reduce-scatter.17.cloned.1.call-done = bf16[1024,512]{1,0:T(8,128)(2,1)} async-done(((bf16[4096,512]{1,0:T(8,128)(2,1)}), bf16[1024,512]{1,0:T(8,128)(2,1)}) %reduce-scatter.17.cloned.1.call-update) | async-done | bytes 1048592 | tf_op jit(solution)/shard_map/reduce_scatter | solution.py:210
  1004.6 6.4 fusion.201
  1013.9 5.9 fusion.269
  1023.8 23.8 %all-gather.15.cloned.1.call-done = bf16[4096,512]{1,0:T(8,128)(2,1)} async-done(((bf16[1024,512]{1,0:T(8,128)(2,1)}), bf16[4096,512]{1,0:T(8,128)(2,1)}) %all-gather.15.cloned.1.call-update) | async-done | bytes 4194320 | tf_op jit(solution)/shard_map/all_gather | solution.py:269
  1057.0 128.5 %while.50 = (s32[]{:T(128)}, bf16[8,1024,3,64]{1,3,2,0:T(8,128)(2,1)}, s32[8,4]{1,0:T(8,128)S(1)}, bf16[8,3,1024,64]{2,3,1,0:T(8,128)(2,1)}, f32[8,1024]{1,0:T(8...) while((s32[]{:T(128)}, bf16[8,1024,3,64]{1,3,2,0:T(8,128)(2,1)}, ...), condition=%wide.region_36.37_spmd, body=%wide.region_31.36_spmd.sunk | while | flops 689820672 | bytes 71097976 | solution.py:277
  1195.0 139.3 %while.51 = (s32[]{:T(128)}, bf16[8,1024,3,64]{1,3,2,0:T(8,128)(2,1)}, s32[8,4]{1,0:T(8,128)}, bf16[8,3,1024,64]{2,3,1,0:T(8,128)(2,1)}, f32[8,1024]{1,0:T(8,128...) while((s32[]{:T(128)}, bf16[8,1024,3,64]{1,3,2,0:T(8,128)(2,1)}, ...), condition=%wide.region_50.51_spmd, body=%wide.region_45.50_spmd.sunk | while | flops 689820672 | bytes 71097976 | solution.py:277
  1334.3 4.3 copy.271
  1353.3 4.7 fusion.160
  1361.5 6.2 convolution_convert_fusion.1
  1367.8 4.4 convolution_convert_fusion
  1378.4 36.9 %reduce-scatter.37.cloned.1.call-done = f32[64,128]{1,0:T(8,128)} async-done(((f32[512,128]{1,0:T(8,128)}), f32[64,128]{1,0:T(8,128)}) %reduce-scatter.37.cloned.1.call-update) | async-done | bytes 32784
  1421.8 60.0 %reduce-scatter.31.cloned.1.call-done = f32[64,2,192]{2,0,1:T(8,128)} async-done(((f32[512,2,192]{2,0,1:T(8,128)}), f32[64,2,192]{2,0,1:T(8,128)}) %reduce-scatter.31.cloned.1.call-update) | async-done | bytes 98320 | tf_op jit(solution)/shard_map/reduce_scatter | solution.py:136
  1488.8 39.1 %reduce-scatter.25.cloned.1.call-done = bf16[1024,512]{1,0:T(8,128)(2,1)} async-done(((bf16[4096,512]{1,0:T(8,128)(2,1)}), bf16[1024,512]{1,0:T(8,128)(2,1)}) %reduce-scatter.25.cloned.1.call-update) | async-done | bytes 1048592 | tf_op jit(solution)/shard_map/reduce_scatter | solution.py:282
  1527.9 47.0 %reduce-scatter.29.cloned.1.call-done = bf16[1024,512]{1,0:T(8,128)(2,1)} async-done(((bf16[4096,512]{1,0:T(8,128)(2,1)}), bf16[1024,512]{1,0:T(8,128)(2,1)}) %reduce-scatter.29.cloned.1.call-update) | async-done | bytes 1048592 | tf_op jit(solution)/shard_map/reduce_scatter | solution.py:282
  1574.9 4.2 fusion.204
  1586.2 40.0 %all-reduce = (f32[4]{0:T(128)}, f32[4]{0:T(128)}, f32[6,512]{1,0:T(8,128)}) all-reduce(f32[4]{0:T(128)} %pad_maximum_fusion.8, f32[4]{0:T(128)} %pad_maximum_fusion.7, f32[6,512]{1,0:T(8,128)} %add.418), channel_id=1, replica_groups=mesh['dp'=8,'tensor'=4] {'dp','tensor'}, use_global_device_ids=true, to_apply=%region_71.72 | all-reduce | flops 3080 | bytes 24640 | tf_op jit(solution)/shard_map/psum | solution.py:332
  1632.5 4.2 fusion.220
  (1260 shorter events, 709.6 us)
Async XLA Ops:
  7.2 74.1 %all-gather.11.cloned.1.call-start = ((), (), s32[]{:S(2)}) async-start(), calls=%async_computation.16 | async-start | bytes 5242880 | tf_op jit(solution)/shard_map/all_gather | solution.py:192
  11.8 37.2 %copy-start.75 = (s32[2,4,4]{2,1,0:T(4,128)S(1)}, s32[2,4,4]{2,1,0:T(4,128)}, u32[]{:S(2)}) copy-start(s32[2,4,4]{2,1,0:T(4,128)} %param.28) | copy-start | bytes 388
  11.8 37.8 %copy-start.41 = (f32[2,64,64]{2,1,0:T(8,128)S(1)}, f32[2,64,64]{2,1,0:T(8,128)}, u32[]{:S(2)}) copy-start(f32[2,64,64]{2,1,0:T(8,128)} %param.30) | copy-start | bytes 98308
  13.8 244.9 %all-gather.7.cloned.1.call-start = ((), (), s32[]{:S(2)}) async-start(), calls=%async_computation.12 | async-start | bytes 5242880 | tf_op jit(solution)/shard_map/all_gather | solution.py:192
  14.5 411.1 %reduce-scatter.19.cloned.1.call-start = ((), (), s32[]{:S(2)}) async-start(), calls=%async_computation.17 | async-start | bytes 10485760 | tf_op jit(solution)/shard_map/reduce_scatter | solution.py:198
  49.0 39.0 %copy-start.31 = (bf16[512,2,192]{0,2,1:T(8,128)(2,1)}, bf16[512,2,192]{0,2,1:T(8,128)(2,1)S(1)}, u32[]{:S(2)}) copy-start(bf16[512,2,192]{0,2,1:T(8,128)(2,1)S(1)} %copy.263) | copy-start | bytes 1179652
  258.4 239.6 %reduce-scatter.15.cloned.1.call-start = ((), (), s32[]{:S(2)}) async-start(), calls=%async_computation.13 | async-start | bytes 10485760 | tf_op jit(solution)/shard_map/reduce_scatter | solution.py:198
  259.4 6.8 copy-start.74
  425.6 72.4 %copy-start.69 = (f32[1,512]{1,0:T(1,128)S(1)}, f32[1,512]{1,0:T(1,128)}, u32[]{:S(2)}) copy-start(f32[1,512]{1,0:T(1,128)} %get-tuple-element.550) | copy-start | bytes 6148
  425.6 201.6 %all-gather.13.cloned.1.call-start = ((), (), s32[]{:S(2)}) async-start(), calls=%async_computation.18 | async-start | bytes 5242880 | tf_op jit(solution)/shard_map/all_gather | solution.py:207
  503.7 134.6 %all-gather.9.cloned.1.call-start = ((), (), s32[]{:S(2)}) async-start(), calls=%async_computation.14 | async-start | bytes 5242880 | tf_op jit(solution)/shard_map/all_gather | solution.py:207
  504.2 212.5 %reduce-scatter.35.cloned.1.call-start = ((), (), s32[]{:S(2)}) async-start(), calls=%async_computation.28 | async-start | bytes 1179648 | tf_op jit(solution)/shard_map/reduce_scatter | solution.py:139
  509.2 41.7 %collective-permute-start = (bf16[1024,512]{1,0:T(8,128)(2,1)}, bf16[1024,512]{1,0:T(8,128)(2,1)}, u32[]{:S(2)}, u32[]{:S(2)}) collective-permute-start(bf16[1024,512]{1,0:T(8,128)(2,1)} %get-tuple-element.469), channel_id=1, source_target_pairs={{0,1},{1,2},{2,3},{3,0},{4,5},{5,6},{6,7},{7,4},{8,9},{9,10},{10,1... | collective-permute-start | bytes 3145736 | tf_op jit(solution)/shard_map/ppermute | solution.py:238
  509.5 72.7 %copy-start.39 = (f32[64,512]{1,0:T(8,128)S(1)}, f32[64,512]{1,0:T(8,128)}, u32[]{:S(2)}) copy-start(f32[64,512]{1,0:T(8,128)} %param.31) | copy-start | bytes 393220
  513.3 68.9 %collective-permute-start.3 = (bf16[1024,512]{1,0:T(8,128)(2,1)}, bf16[1024,512]{1,0:T(8,128)(2,1)S(1)}, u32[]{:S(2)}, u32[]{:S(2)}) collective-permute-start(bf16[1024,512]{1,0:T(8,128)(2,1)} %get-tuple-element.471), channel_id=1, source_target_pairs={{0,1},{1,2},{2,3},{3,0},{4,5},{5,6},{6,7},{7,4},{8,9},{9,10},{10,1... | collective-permute-start | bytes 3145736 | tf_op jit(solution)/shard_map/ppermute | solution.py:238
  514.2 102.8 %collective-permute-start.1 = (bf16[1024,512]{1,0:T(8,128)(2,1)}, bf16[1024,512]{1,0:T(8,128)(2,1)}, u32[]{:S(2)}, u32[]{:S(2)}) collective-permute-start(bf16[1024,512]{1,0:T(8,128)(2,1)} %get-tuple-element.469), channel_id=1, source_target_pairs={{0,3},{1,0},{2,1},{3,2},{4,7},{5,4},{6,5},{7,6},{8,11},{9,8},{10,9... | collective-permute-start | bytes 3145736 | tf_op jit(solution)/shard_map/ppermute | solution.py:246
  515.6 103.7 %collective-permute-start.4 = (bf16[1024,512]{1,0:T(8,128)(2,1)}, bf16[1024,512]{1,0:T(8,128)(2,1)}, u32[]{:S(2)}, u32[]{:S(2)}) collective-permute-start(bf16[1024,512]{1,0:T(8,128)(2,1)} %get-tuple-element.471), channel_id=1, source_target_pairs={{0,3},{1,0},{2,1},{3,2},{4,7},{5,4},{6,5},{7,6},{8,11},{9,8},{10,9... | collective-permute-start | bytes 3145736 | tf_op jit(solution)/shard_map/ppermute | solution.py:246
  550.9 70.6 %collective-permute-start.2 = (bf16[1024,512]{1,0:T(8,128)(2,1)}, bf16[1024,512]{1,0:T(8,128)(2,1)}, u32[]{:S(2)}, u32[]{:S(2)}) collective-permute-start(bf16[1024,512]{1,0:T(8,128)(2,1)} %collective-permute-done), channel_id=1, source_target_pairs={{0,1},{1,2},{2,3},{3,0},{4,5},{5,6},{6,7},{7,4},{8,9},{9,10},{10,1... | collective-permute-start | bytes 3145736 | tf_op jit(solution)/shard_map/ppermute | solution.py:238
  582.2 42.7 %collective-permute-start.5 = (bf16[1024,512]{1,0:T(8,128)(2,1)S(1)}, bf16[1024,512]{1,0:T(8,128)(2,1)}, u32[]{:S(2)}, u32[]{:S(2)}) collective-permute-start(bf16[1024,512]{1,0:T(8,128)(2,1)S(1)} %collective-permute-done.3), channel_id=1, source_target_pairs={{0,1},{1,2},{2,3},{3,0},{4,5},{5,6},{6,7},{7,4},{8,9},{9,10},{10,1... | collective-permute-start | bytes 3145736 | tf_op jit(solution)/shard_map/ppermute | solution.py:238
  627.2 8.7 copy-start.26
  646.8 70.0 %copy-start.43 = (f32[512,64]{0,1:T(8,128)S(1)}, f32[512,64]{0,1:T(8,128)}, u32[]{:S(2)}) copy-start(f32[512,64]{0,1:T(8,128)} %param.32) | copy-start | bytes 393220
  646.8 70.0 %copy-start.51 = (f32[512,64]{0,1:T(8,128)S(1)}, f32[512,64]{0,1:T(8,128)}, u32[]{:S(2)}) copy-start(f32[512,64]{0,1:T(8,128)} %param.40) | copy-start | bytes 393220
  646.8 70.0 %copy-start.52 = (f32[512,64]{0,1:T(8,128)S(1)}, f32[512,64]{0,1:T(8,128)}, u32[]{:S(2)}) copy-start(f32[512,64]{0,1:T(8,128)} %param.41) | copy-start | bytes 393220
  652.4 184.0 %reduce-scatter.23.cloned.1.call-start = ((), (), s32[]{:S(2)}) async-start(), calls=%async_computation.20 | async-start | bytes 10485760 | tf_op jit(solution)/shard_map/reduce_scatter | solution.py:261
  766.2 144.3 %reduce-scatter.27.cloned.1.call-start = ((), (), s32[]{:S(2)}) async-start(), calls=%async_computation.23 | async-start | bytes 10485760 | tf_op jit(solution)/shard_map/reduce_scatter | solution.py:261
  782.4 175.0 %reduce-scatter.21.cloned.1.call-start = ((), (), s32[]{:S(2)}) async-start(), calls=%async_computation.19 | async-start | bytes 5242880 | tf_op jit(solution)/shard_map/reduce_scatter | solution.py:210
  789.1 215.5 %reduce-scatter.17.cloned.1.call-start = ((), (), s32[]{:S(2)}) async-start(), calls=%async_computation.15 | async-start | bytes 5242880 | tf_op jit(solution)/shard_map/reduce_scatter | solution.py:210
  795.8 114.6 %copy-start.9 = (f32[1024,512]{1,0:T(8,128)S(1)}, f32[1024,512]{1,0:T(8,128)}, u32[]{:S(2)}) copy-start(f32[1024,512]{1,0:T(8,128)} %copy-done.8) | copy-start | bytes 6291460
  795.9 251.8 %all-gather.15.cloned.1.call-start = ((), (), s32[]{:S(2)}) async-start(), calls=%async_computation.21 | async-start | bytes 5242880 | tf_op jit(solution)/shard_map/all_gather | solution.py:269
  957.4 47.2 %copy-start.30 = (bf16[1024,512]{1,0:T(8,128)(2,1)S(1)}, bf16[1024,512]{1,0:T(8,128)(2,1)}, u32[]{:S(2)}) copy-start(bf16[1024,512]{1,0:T(8,128)(2,1)} %reduce-scatter.21.cloned.1.call-done) | copy-start | bytes 3145732
  1004.6 6.4 copy-start.16
  1013.0 172.5 %all-gather.17.cloned.1.call-start = ((), (), s32[]{:S(2)}) async-start(), calls=%async_computation.24 | async-start | bytes 5242880 | tf_op jit(solution)/shard_map/all_gather | solution.py:269
  1013.8 358.5 %reduce-scatter.33.cloned.1.call-start = ((), (), s32[]{:S(2)}) async-start(), calls=%async_computation.27 | async-start | bytes 1179648 | tf_op jit(solution)/shard_map/reduce_scatter | solution.py:138
  1013.8 6.0 copy-start.13
  1013.8 6.1 copy-start.24
  1023.3 392.0 %reduce-scatter.37.cloned.1.call-start = ((), (), s32[]{:S(2)}) async-start(), calls=%async_computation.29 | async-start | bytes 294912
  1353.1 128.8 %reduce-scatter.31.cloned.1.call-start = ((), (), s32[]{:S(2)}) async-start(), calls=%async_computation.26 | async-start | bytes 1179648 | tf_op jit(solution)/shard_map/reduce_scatter | solution.py:136
  1361.5 166.4 %reduce-scatter.25.cloned.1.call-start = ((), (), s32[]{:S(2)}) async-start(), calls=%async_computation.22 | async-start | bytes 5242880 | tf_op jit(solution)/shard_map/reduce_scatter | solution.py:282
  1367.8 207.1 %reduce-scatter.29.cloned.1.call-start = ((), (), s32[]{:S(2)}) async-start(), calls=%async_computation.25 | async-start | bytes 5242880 | tf_op jit(solution)/shard_map/reduce_scatter | solution.py:282
  1372.2 44.1 %copy-start.42 = (f32[2,64,64]{2,1,0:T(8,128)S(1)}, f32[2,64,64]{2,1,0:T(8,128)}, u32[]{:S(2)}) copy-start(f32[2,64,64]{2,1,0:T(8,128)} %param.30) | copy-start | bytes 98308
  1372.2 109.6 %copy-start.38 = (f32[64,2,192]{2,1,0:T(2,128)S(1)}, f32[64,2,192]{2,1,0:T(2,128)}, u32[]{:S(2)}) copy-start(f32[64,2,192]{2,1,0:T(2,128)} %param.29) | copy-start | bytes 294916
  1375.5 199.4 %copy-start.7 = (bf16[2,1024,512]{2,1,0:T(8,128)(2,1)S(1)}, bf16[2,1024,512]{2,1,0:T(8,128)(2,1)}, u32[]{:S(2)}) copy-start(bf16[2,1024,512]{2,1,0:T(8,128)(2,1)} %param.26) | copy-start | bytes 6291460
  1375.5 199.4 %copy-start.57 = (f32[1024]{0:T(1024)S(1)}, f32[1024]{0:T(1024)}, u32[]{:S(2)}) copy-start(f32[1024]{0:T(1024)} %copy-done.56) | copy-start | bytes 12292
  1375.5 199.4 %copy-start.59 = (f32[1024]{0:T(1024)S(1)}, f32[1024]{0:T(1024)}, u32[]{:S(2)}) copy-start(f32[1024]{0:T(1024)} %copy-done.58) | copy-start | bytes 12292
  1375.5 199.3 %copy-start.63 = (f32[1024]{0:T(1024)S(1)}, f32[1024]{0:T(1024)}, u32[]{:S(2)}) copy-start(f32[1024]{0:T(1024)} %copy-done.62) | copy-start | bytes 12292
  1375.5 199.3 %copy-start.65 = (f32[1024]{0:T(1024)S(1)}, f32[1024]{0:T(1024)}, u32[]{:S(2)}) copy-start(f32[1024]{0:T(1024)} %copy-done.64) | copy-start | bytes 12292
  1418.5 220.7 %copy-start.49 = (f32[2,64,64]{2,1,0:T(8,128)}, f32[2,64,64]{2,1,0:T(8,128)S(1)}, u32[]{:S(2)}) copy-start(f32[2,64,64]{2,1,0:T(8,128)S(1)} %get-tuple-element.462) | copy-start | bytes 98308
  1527.9 104.6 %copy-start.28 = (bf16[1024,512]{1,0:T(8,128)(2,1)S(1)}, bf16[1024,512]{1,0:T(8,128)(2,1)}, u32[]{:S(2)}) copy-start(bf16[1024,512]{1,0:T(8,128)(2,1)} %reduce-scatter.25.cloned.1.call-done) | copy-start | bytes 3145732
  (110 other events, 322.0 us)
Sparse Core Ops, SparseCore 0:
  13.9 37.1 all-gather.10
  53.2 34.4 all-gather.6
  258.5 72.3 reduce-scatter.18
  425.7 72.1 reduce-scatter.14
  503.8 55.9 all-gather.12
  561.2 51.2 all-gather.8
  652.5 64.1 reduce-scatter.34
  766.3 70.0 reduce-scatter.22
  839.1 71.3 reduce-scatter.26
  912.9 44.5 reduce-scatter.20
  960.0 44.5 reduce-scatter.16
  1013.2 34.4 all-gather.14
  1049.2 34.4 all-gather.16
  1086.9 64.2 reduce-scatter.32
  1353.2 62.1 reduce-scatter.36
  1418.6 63.1 reduce-scatter.30
  1484.2 43.6 reduce-scatter.24
  1530.2 44.5 reduce-scatter.28
